TPU v7x, 128 devices: a whole 4x4x4 slice. The times are simulated.
128 devices in a mesh: dp: 4 (over x_lo, core), expert: 32 (over y, x_hi, z).
Axes of the slice: x: 4 (x_hi: 2, x_lo: 2; x = x_hi * 2 + x_lo), y: 4, z: 4, core: 2. Of those that a mesh axis runs over, the one named last changes fastest.
Arguments:
- hidden_in: bfloat16 [16384, 2048], P(('dp', 'expert')), may hold values from -6 to 6
- attn_gain: float32 [2048], replicated, may hold values from 0.1 to 1.9
- query_key_value_weight: bfloat16 [2048, 2560], P('expert'), may hold values from -0.125 to 0.125
- q_gain: float32 [128], replicated, may hold values from 0.1 to 1.9
- key_norm_gain: float32 [128], replicated, may hold values from 0.1 to 1.9
- w_out: bfloat16 [2048, 2048], P('expert'), may hold values from -0.125 to 0.125
- moe_gain: float32 [2048], replicated, may hold values from 0.1 to 1.9
- w_gate_up: bfloat16 [128, 2048, 1536], P(('dp', 'expert')), may hold values from -0.125 to 0.125
- w_down: bfloat16 [128, 768, 2048], P(('dp', 'expert')), may hold values from -0.21875 to 0.21875
- kv_pool: bfloat16 [32, 2, 128, 2, 128], P('dp'), may hold values from -160 to 160
- page_table: int32 [32], replicated, may hold values from 0 to 31, each once
- suffix_lengths: int32 [4, 4], replicated, may hold values from 1 to 2560, 4096 in all within a row
- request_group: int32 [4, 4], replicated, may hold values from 0 to 1
- expert_ids: int32 [16384, 8], P(('dp', 'expert')), may hold values from 0 to 127, all different within a row; in each aligned block of 128 rows (0 to 127, 128 to 255, ...) at most 12 rows name the same one
- gate_weights: float32 [16384, 8], P(('dp', 'expert')), may hold values from 0.05 to 0.3
Outputs:
- hidden_out: bfloat16 [16384, 2048], P(('dp', 'expert'))
- suffix_cache: bfloat16 [16384, 512], P(('dp', 'expert'))
Inputs may be any that keep to these rules, and one draw needn't show every extreme that they name: page_table holds each pool page once. `suffix_lengths`: each row sums to 4096; the largest of each row is exactly 2560. `expert_ids`: a token's 8 experts differ; among the 128 rows of one device no expert is named more than 12 times, and that many times in some device.
All inputs are finite; a program needn't handle non-finite values.
Results may differ from a plain program's by a relative error of at most 0.01.
The roundings to bfloat16 on the way count: a program that leaves them out, or rounds other values in their place, can miss the bound.
Values may be sent and summed in bfloat16 or wider, within the bound.
A program may use at most 256 MiB of HBM per device.

v0:
```python
import math
import jax
import jax.numpy as jnp
from jax import lax
from jax.sharding import PartitionSpec as P

PREFIX_TOKENS = 2048
PAGE_TOKENS = 128
eps = 1e-06
theta = 1000000.0
floor_value = -1e30


def root_mean_scale(value_rows, gain):
    value_rows = value_rows.astype(jnp.float32)
    return (
        value_rows
        * lax.rsqrt(jnp.mean(value_rows * value_rows, axis=-1, keepdims=True) + eps)
        * gain
    )


def rotary_apply(value_rows, token_positions):
    half = value_rows.shape[-1] // 2
    freqs = theta ** (-jnp.arange(half, dtype=jnp.float32) / half)
    angles = token_positions.astype(jnp.float32)[:, None] * freqs[None, :]
    cosine = jnp.cos(angles)[:, None, :]
    sine = jnp.sin(angles)[:, None, :]
    first = value_rows[..., :half]
    second_split = value_rows[..., half:]
    return jnp.concatenate(
        [first * cosine - second_split * sine, second_split * cosine + first * sine], axis=-1
    )


def layout(lengths_row, index):
    ends = jnp.cumsum(lengths_row)
    starts = ends - lengths_row
    request = jnp.sum((index[:, None] >= ends[None, :]).astype(jnp.int32), axis=1)
    chosen = request[:, None] == jnp.arange(lengths_row.shape[0], dtype=jnp.int32)[None, :]
    offset = index - jnp.sum(jnp.where(chosen, starts[None, :], 0), axis=1)
    return (request, offset, chosen)


def attend(carry, queries, key_rows, value_rows, mask, scale):
    high, total, acc = carry
    scores = (
        jnp.einsum("qkgd,skd->kgqs", queries, key_rows, preferred_element_type=jnp.float32) * scale
    )
    scores = jnp.where(mask[None, None], scores, -jnp.inf)
    new_high = jnp.maximum(high, jnp.max(scores, axis=-1))
    weights = jnp.exp(scores - new_high[..., None])
    scale_factor = jnp.exp(high - new_high)
    total = total * scale_factor + jnp.sum(weights, axis=-1)
    acc = acc * scale_factor[..., None] + jnp.einsum(
        "kgqs,skd->kgqd",
        weights.astype(jnp.bfloat16),
        value_rows,
        preferred_element_type=jnp.float32,
    )
    return (new_high, total, acc)


def expert_rows(rows, gate_up, down):
    both = jnp.dot(rows, gate_up, preferred_element_type=jnp.float32)
    half = both.shape[1] // 2
    act = (jax.nn.silu(both[:, :half]) * both[:, half:]).astype(jnp.bfloat16)
    return jnp.dot(act, down, preferred_element_type=jnp.float32).astype(jnp.bfloat16)


def local(
    hidden_in,
    attn_gain,
    query_key_value_weight,
    q_gain,
    key_norm_gain,
    w_out,
    moe_gain,
    w_gate_up,
    w_down,
    kv_pool,
    page_table,
    suffix_lengths,
    request_group,
    expert_ids,
    gate_weights,
):
    tokens_here, width = hidden_in.shape
    page_rows = kv_pool.shape[2]
    kv_heads = kv_pool.shape[3]
    head_dim = kv_pool.shape[4]
    key_value_width = kv_heads * head_dim
    query_width = query_key_value_weight.shape[1] - 2 * key_value_width
    q_heads = query_width // head_dim
    head_split = q_heads // kv_heads
    scale = 1.0 / math.sqrt(head_dim)
    row_count = lax.axis_size("dp")
    col_count = lax.axis_size("expert")
    row = lax.axis_index("dp")
    col = lax.axis_index("expert")
    normed = root_mean_scale(hidden_in, attn_gain).astype(jnp.bfloat16)
    part = normed
    qkv = jnp.dot(
        part,
        lax.all_gather(query_key_value_weight, "expert", axis=0, tiled=True),
        preferred_element_type=jnp.float32,
    )
    index = col * tokens_here + jnp.arange(tokens_here, dtype=jnp.int32)
    lengths_row = lax.dynamic_index_in_dim(suffix_lengths, row, 0, keepdims=False)
    groups_row = lax.dynamic_index_in_dim(request_group, row, 0, keepdims=False)
    request, offset, chosen = layout(lengths_row, index)
    qgroup = jnp.sum(jnp.where(chosen, groups_row[None, :], 0), axis=1)
    token_positions = PREFIX_TOKENS + offset
    queries = rotary_apply(
        root_mean_scale(qkv[:, :query_width].reshape(tokens_here, q_heads, head_dim), q_gain),
        token_positions,
    ).astype(jnp.bfloat16)
    key_rows = rotary_apply(
        root_mean_scale(
            qkv[:, query_width : query_width + key_value_width].reshape(
                tokens_here, kv_heads, head_dim
            ),
            key_norm_gain,
        ),
        token_positions,
    ).astype(jnp.bfloat16)
    value_rows = (
        qkv[:, query_width + key_value_width :]
        .reshape(tokens_here, kv_heads, head_dim)
        .astype(jnp.bfloat16)
    )
    suffix_cache = jnp.concatenate(
        [
            key_rows.reshape(tokens_here, key_value_width),
            value_rows.reshape(tokens_here, key_value_width),
        ],
        axis=1,
    )
    grouped = queries.reshape(tokens_here, kv_heads, head_split, head_dim)
    carry = (
        jnp.full((kv_heads, head_split, tokens_here), floor_value, jnp.float32),
        jnp.zeros((kv_heads, head_split, tokens_here), jnp.float32),
        jnp.zeros((kv_heads, head_split, tokens_here, head_dim), jnp.float32),
    )
    piece_keys = lax.all_gather(key_rows, "expert", axis=0, tiled=True)
    piece_values = lax.all_gather(value_rows, "expert", axis=0, tiled=True)
    key_index = jnp.arange(piece_keys.shape[0], dtype=jnp.int32)
    key_request, _, _ = layout(lengths_row, key_index)
    mask = (key_request[None, :] == request[:, None]) & (key_index[None, :] <= index[:, None])
    carry = attend(carry, grouped, piece_keys, piece_values, mask, scale)
    per_group = PREFIX_TOKENS // PAGE_TOKENS
    slot_ids = jnp.arange(page_table.shape[0], dtype=jnp.int32)
    piece = lax.all_gather(kv_pool, "dp", axis=0, tiled=True)
    count = piece.shape[0]
    hit = page_table[None, :] == jnp.arange(count, dtype=jnp.int32)[:, None]
    key_group = jnp.repeat(
        jnp.sum(jnp.where(hit, slot_ids[None, :] // per_group, 0), axis=1), page_rows
    )
    mask = key_group[None, :] == qgroup[:, None]
    carry = attend(
        carry,
        grouped,
        piece[:, 0].reshape(count * page_rows, kv_heads, head_dim),
        piece[:, 1].reshape(count * page_rows, kv_heads, head_dim),
        mask,
        scale,
    )
    mixed = (
        (carry[2] / carry[1][..., None])
        .transpose(2, 0, 1, 3)
        .reshape(tokens_here, query_width)
        .astype(jnp.bfloat16)
    )
    part = mixed
    projected = jnp.dot(
        part,
        lax.all_gather(w_out, "expert", axis=0, tiled=True),
        preferred_element_type=jnp.float32,
    )
    mid = (hidden_in.astype(jnp.float32) + projected).astype(jnp.bfloat16)
    moe_in = root_mean_scale(mid, moe_gain).astype(jnp.bfloat16)
    top_k = expert_ids.shape[1]
    expert_count = row_count * col_count
    capacity = max(2, tokens_here * top_k * 3 // (2 * expert_count))
    flat = expert_ids.reshape(-1)
    onehot = (flat[:, None] == jnp.arange(expert_count, dtype=jnp.int32)[None, :]).astype(jnp.int32)
    slot = jnp.sum((jnp.cumsum(onehot, axis=0) - onehot) * onehot, axis=1)
    place = flat * capacity + slot
    sources = jnp.repeat(moe_in, top_k, axis=0)
    outgoing = jnp.zeros((expert_count * capacity, width), jnp.bfloat16).at[place].set(sources)
    gate_up = w_gate_up[0]
    down = w_down[0]
    received = lax.all_to_all(
        outgoing.reshape(expert_count, capacity, width),
        ("dp", "expert"),
        split_axis=0,
        concat_axis=0,
        tiled=True,
    )
    results = expert_rows(received.reshape(-1, width), gate_up, down).reshape(received.shape)
    returned = lax.all_to_all(results, ("dp", "expert"), split_axis=0, concat_axis=0, tiled=True)
    picked = returned.reshape(expert_count * capacity, width)[place].astype(jnp.float32)
    moe = jnp.sum(picked.reshape(tokens_here, top_k, width) * gate_weights[:, :, None], axis=1)
    hidden_out = (mid.astype(jnp.float32) + moe).astype(jnp.bfloat16)
    return (hidden_out, suffix_cache)


def solution(mesh):
    return jax.shard_map(
        local,
        mesh=mesh,
        in_specs=(
            P(("dp", "expert"), None),
            P(),
            P("expert", None),
            P(),
            P(),
            P("expert", None),
            P(),
            P(("dp", "expert"), None, None),
            P(("dp", "expert"), None, None),
            P("dp", None, None, None, None),
            P(),
            P(),
            P(),
            P(("dp", "expert"), None),
            P(("dp", "expert"), None),
        ),
        out_specs=(P(("dp", "expert"), None), P(("dp", "expert"), None)),
        check_vma=False,
    )
```

profile of v0, /device:TPU:67, one launch (start us, length us, event | category | flops | bytes accessed | tf_op | source)
XLA Modules:
  0.0 756.2 jit_solution(2184994517330569896)
XLA Ops:
  8.0 2.6 copy.97
  12.4 1.2 fusion.65
  14.0 114.5 %all-gather.6.cloned.1.call-done = bf16[2048,2560]{1,0:T(8,128)(2,1)} async-done(((bf16[64,2560]{1,0:T(8,128)(2,1)}), bf16[2048,2560]{1,0:T(8,128)(2,1)}) %all-gather.6.cloned.1.call-update) | async-done | bytes 10485776 | tf_op jit(solution)/shard_map/all_gather | solution.py:105
  128.5 5.7 fusion.68
  134.3 1.1 copy-done.8
  136.0 1.6 reshape.345
  137.7 1.1 multiply_reduce_fusion.2
  140.6 0.9 slice.85
  143.5 0.8 copy-done.11
  144.3 1.9 broadcast_add_fusion
  146.4 1.9 copy.104
  148.5 1.4 fusion.71
  150.1 1.2 broadcast_compare_fusion
  151.2 3.1 fusion.29
  154.3 21.2 %all-gather.12.cloned.1.call-done = bf16[32,2,128,2,128]{4,2,3,1,0:T(8,128)(2,1)} async-done(((bf16[8,2,128,2,128]{4,2,3,1,0:T(8,128)(2,1)}), bf16[32,2,128,2,128]{4,2,3,1,0:T(8,128)(2,1)}) %all-gather.12.cloned.1.call-update) | async-done | bytes 4194320 | tf_op jit(solution)/shard_map/all_gather | solution.py:153
  175.5 4.1 fusion.94
  179.6 1.6 copy.98
  181.2 4.6 copy.99
  185.8 4.2 reshape.374
  190.0 1.3 slice_bitcast_fusion
  191.5 1.0 copy-done.6
  193.1 1.7 multiply_multiply_fusion
  196.5 13.6 %bitcast_reduce_fusion = (f32[2,8,128]{2,1,0:T(8,128)S(1)}, f32[2,128,8,4096]{3,1,2,0:T(8,128)}) fusion(pred[128,4096]{1,0:T(8,128)(4,1)S(1)} %copy-done.2, bf16[4096,2,128,1]{2,0,3,1:T(8,128)(2,1)S(1)} %bitcast.168, bf16[128,2,8,64]{3,0,2,1:T(8,128)(2,1)S(1)} %bitcast.171, bf16[128,2,8,64]{3,0,2,1:T(8,128)(2,1)S(1)} %bitcast.169), kind=kOutput, calls=%fused_computation.3 | convolution fusion | flops 2173696000 | bytes 36708352 | tf_op jit(solution)/shard_map/qkgd,skd->kgqs/dot_general | solution.py:48
  210.1 38.8 %all-gather.8.cloned.1.call-done = bf16[4096,2,128]{2,0,1:T(8,128)(2,1)} async-done(((bf16[128,2,128]{2,0,1:T(8,128)(2,1)}), bf16[4096,2,128]{2,0,1:T(8,128)(2,1)}) %all-gather.8.cloned.1.call-update) | async-done | bytes 2097168 | tf_op jit(solution)/shard_map/all_gather | solution.py:145
  249.0 15.0 %fusion.3 = (f32[2,8,128]{2,1,0:T(8,128)S(1)}, f32[2,4096,128,8]{2,1,3,0:T(8,128)}) fusion(pred[128,4096]{0,1:T(8,128)(4,1)} %fusion.29, bf16[128,2,8,64]{3,0,2,1:T(8,128)(2,1)} %bitcast.172, bf16[128,2,8,64]{3,0,2,1:T(8,128)(2,1)} %bitcast.170, bf16[4096,2,128]{2,0,1:T(8,128)(2,1)} %all-gather.8.cloned.1.call-done), kind=kOutput, calls=%fused_computation.10 | convolution fusion | flops 2173696000 | bytes 36708352 | tf_op jit(solution)/shard_map/qkgd,skd->kgqs/dot_general | solution.py:48
  264.0 16.4 %fusion.1 = f32[2,8,128]{2,1,0:T(8,128)S(1)} fusion(f32[2,4096,128,8]{2,1,3,0:T(8,128)} %get-tuple-element.22, f32[2,8,128]{2,1,0:T(8,128)S(1)} %get-tuple-element.16, pred[128,4096]{0,1:T(8,128)(4,1)S(1)} %copy-done.4), kind=kLoop, calls=%fused_computation.8 | loop fusion | flops 33552384 | bytes 34095104 | tf_op jit(solution)/shard_map/reduce_sum | solution.py:54
  280.3 3.9 copy-done.1
  284.2 9.5 %fusion.4 = f32[2,8,128]{2,1,0:T(8,128)S(1)} fusion(f32[2,128,8,4096]{3,1,2,0:T(8,128)S(1)} %copy-done.1, f32[2,8,128]{2,1,0:T(8,128)S(1)} %get-tuple-element.15, pred[128,4096]{1,0:T(8,128)(4,1)S(1)} %copy-done.3), kind=kLoop, calls=%fused_computation.11 | loop fusion | flops 33552384 | bytes 34095104 | tf_op jit(solution)/shard_map/reduce_sum | solution.py:54
  293.8 28.9 %all-gather.10.cloned.1.call-done = bf16[4096,2,128]{0,2,1:T(8,128)(2,1)} async-done(((bf16[128,2,128]{0,2,1:T(8,128)(2,1)}), bf16[4096,2,128]{0,2,1:T(8,128)(2,1)}) %all-gather.10.cloned.1.call-update) | async-done | bytes 2097168 | tf_op jit(solution)/shard_map/all_gather | solution.py:146
  322.7 16.3 %fusion.50 = f32[128,2,8,128]{0,3,2,1:T(8,128)} fusion(f32[2,4096,128,8]{2,1,3,0:T(8,128)} %get-tuple-element.22, f32[2,8,128]{2,1,0:T(8,128)S(1)} %get-tuple-element.16, pred[128,4096]{0,1:T(8,128)(4,1)} %fusion.29, bf16[4096,2,128]{0,2,1:T(8,128)(2,1)} %all-gather.10.cloned.1.call-done, f32[128,2,8]{0,2,1:T(8,128)S(1)} %get-tuple-element.5, ...), kind=kOutput, calls=%fused_computation.45 | convolution fusion | flops 2181562368 | bytes 37249024 | tf_op jit(solution)/shard_map/kgqs,skd->kgqd/dot_general | solution.py:55
  339.0 16.3 %fusion.60 = bf16[128,2,8,128]{0,3,2,1:T(8,128)(2,1)} fusion(f32[128,2,8,128]{0,3,2,1:T(8,128)} %fusion.50, bf16[4096,2,128,1]{0,2,1,3:T(8,128)(2,1)} %reshape.374, f32[2,128,8,4096]{3,1,2,0:T(8,128)} %get-tuple-element.20, f32[2,8,128]{2,1,0:T(8,128)S(1)} %get-tuple-element.15, pred[128,4096]{1,0:T(8,128)(4,1)} %broadcast_compare_fusion, ...), kind=kOutput, calls=%fused_computation.47 | convolution fusion | flops 2181824512 | bytes 37765120 | tf_op jit(solution)/shard_map/kgqs,skd->kgqd/dot_general | solution.py:55
  355.4 73.6 %all-gather.14.cloned.1.call-done = bf16[2048,2048]{1,0:T(8,128)(2,1)} async-done(((bf16[64,2048]{1,0:T(8,128)(2,1)}), bf16[2048,2048]{1,0:T(8,128)(2,1)}) %all-gather.14.cloned.1.call-update) | async-done | bytes 8388624 | tf_op jit(solution)/shard_map/all_gather | solution.py:177
  429.0 4.9 multiply_reduce_fusion
  433.9 1.0 copy-done.5
  434.9 0.9 multiply_convert_fusion
  435.9 10.9 %scatter_custom_fusion = bf16[1536,2048]{1,0:T(8,128)(2,1)} fusion(s32[1024]{0:T(1024)S(1)} %bitcast.176, bf16[]{:T(256)} %constant.80.clone.1, bf16[128,2048]{1,0:T(8,128)(2,1)} %multiply_convert_fusion), kind=kCustom, calls=%fused_computation.24 | custom fusion | bytes 6815746 | tf_op jit(solution)/shard_map/scatter | solution.py:190
  446.8 10.6 %reshape.350 = bf16[128,12,2048]{2,1,0:T(8,128)(2,1)} reshape(bf16[1536,2048]{1,0:T(8,128)(2,1)} %scatter_custom_fusion) | data formatting | bytes 12582912 | tf_op jit(solution)/shard_map/reshape | solution.py:194
  457.4 105.0 %all_to_all.10 = bf16[128,12,2048]{2,1,0:T(8,128)(2,1)} all-to-all(bf16[128,12,2048]{2,1,0:T(8,128)(2,1)} %reshape.350), channel_id=1, replica_groups=mesh['dp'=4,'expert'=32] {'dp','expert'}, dimensions={0} | all-to-all | bytes 12582912 | tf_op jit(solution)/shard_map/all_to_all | solution.py:193
  562.4 10.7 %reshape.351 = bf16[1536,2048]{1,0:T(8,128)(2,1)} reshape(bf16[128,12,2048]{2,1,0:T(8,128)(2,1)} %all_to_all.10) | data formatting | bytes 12582912 | tf_op jit(solution)/shard_map/reshape | solution.py:200
  573.1 14.1 %fusion.13 = f32[1536,1536]{1,0:T(8,128)S(1)} fusion(bf16[1536,2048]{1,0:T(8,128)(2,1)} %reshape.351, bf16[1,2048,1536]{2,1,0:T(8,128)(2,1)} %param.22), kind=kOutput, calls=%fused_computation.20 | convolution fusion | flops 9663676416 | bytes 22020096 | tf_op jit(solution)/shard_map/dot_general | solution.py:65
  587.3 7.1 convolution_convert_fusion
  594.3 10.6 %reshape.352 = bf16[128,12,2048]{2,1,0:T(8,128)(2,1)} reshape(bf16[1536,2048]{1,0:T(8,128)(2,1)} %convolution_convert_fusion) | data formatting | bytes 12582912 | tf_op jit(solution)/shard_map/reshape | solution.py:200
  604.9 7.6 %all-to-all-start.1 = ((bf16[128,12,2048]{2,1,0:T(8,128)(2,1)}), bf16[128,12,2048]{2,1,0:T(8,128)(2,1)}, u32[]{:S(2)}, u32[]{:S(2)}) async-start(bf16[128,12,2048]{2,1,0:T(8,128)(2,1)} %reshape.352), calls=%async_computation.1 | async-start | bytes 16777216 | tf_op jit(solution)/shard_map/all_to_all | solution.py:201
  613.5 104.1 %all-to-all-done.1 = bf16[128,12,2048]{2,1,0:T(8,128)(2,1)} async-done(((bf16[128,12,2048]{2,1,0:T(8,128)(2,1)}), bf16[128,12,2048]{2,1,0:T(8,128)(2,1)}, u32[]{:S(2)}, u32[]{:S(2)}) %all-to-all-start.1) | async-done | bytes 6291488 | tf_op jit(solution)/shard_map/all_to_all | solution.py:201
  717.5 10.7 %reshape.353 = bf16[1536,2048]{1,0:T(8,128)(2,1)} reshape(bf16[128,12,2048]{2,1,0:T(8,128)(2,1)} %all-to-all-done.1) | data formatting | bytes 12582912 | tf_op jit(solution)/shard_map/reshape | solution.py:202
  728.2 12.4 %gather_fusion = bf16[1024,2048]{1,0:T(8,128)(2,1)} fusion(bf16[1536,2048]{1,0:T(8,128)(2,1)} %reshape.353, s32[1024]{0:T(1024)S(1)} %broadcast_clamp_fusion), kind=kCustom, calls=%fused_computation | custom fusion | bytes 8392704 | tf_op jit(solution)/shard_map/gather | solution.py:202
  740.7 6.5 fusion.12
  747.2 2.2 add_convert_fusion
  (101 shorter events, 11.1 us)
Async XLA Ops:
  7.2 580.1 %copy-start = (bf16[1,768,2048]{2,1,0:T(8,128)(2,1)S(1)}, bf16[1,768,2048]{2,1,0:T(8,128)(2,1)}, u32[]{:S(2)}) copy-start(bf16[1,768,2048]{2,1,0:T(8,128)(2,1)} %param.23) | copy-start | bytes 9437188
  7.2 121.3 %all-gather.6.cloned.1.call-start = ((), (), s32[]{:S(2)}) async-start(), calls=%async_computation.2 | async-start | bytes 10813440 | tf_op jit(solution)/shard_map/all_gather | solution.py:105
  7.9 167.6 %all-gather.12.cloned.1.call-start = ((), (), s32[]{:S(2)}) async-start(), calls=%async_computation.5 | async-start | bytes 5242880 | tf_op jit(solution)/shard_map/all_gather | solution.py:153
  10.6 238.4 %all-gather.8.cloned.1.call-start = ((), (), s32[]{:S(2)}) async-start(), calls=%async_computation.3 | async-start | bytes 2162688 | tf_op jit(solution)/shard_map/all_gather | solution.py:145
  14.0 124.9 %copy-start.21 = (f32[128]{0:T(128)S(1)}, f32[128]{0:T(128)}, u32[]{:S(2)}) copy-start(f32[128]{0:T(128)} %param.19) | copy-start | bytes 1540
  14.0 129.0 %copy-start.18 = (s32[128,8]{0,1:T(8,128)S(1)}, s32[128,8]{0,1:T(8,128)}, u32[]{:S(2)}) copy-start(s32[128,8]{0,1:T(8,128)} %param.28) | copy-start | bytes 12292
  14.0 132.2 %copy-start.23 = (s32[32]{0:T(128)S(1)}, s32[32]{0:T(128)}, u32[]{:S(2)}) copy-start(s32[32]{0:T(128)} %param.25) | copy-start | bytes 388
  134.3 1.1 copy-start.8
  139.1 0.6 copy-start.12
  139.1 0.6 copy-start.14
  140.5 182.2 %all-gather.10.cloned.1.call-start = ((), (), s32[]{:S(2)}) async-start(), calls=%async_computation.4 | async-start | bytes 2162688 | tf_op jit(solution)/shard_map/all_gather | solution.py:146
  141.5 1.4 copy-start.16
  142.2 286.7 %all-gather.14.cloned.1.call-start = ((), (), s32[]{:S(2)}) async-start(), calls=%async_computation.6 | async-start | bytes 8650752 | tf_op jit(solution)/shard_map/all_gather | solution.py:177
  143.5 0.8 copy-start.11
  179.5 13.5 %copy-start.22 = (f32[128]{0:T(128)S(1)}, f32[128]{0:T(128)}, u32[]{:S(2)}) copy-start(f32[128]{0:T(128)} %param.18) | copy-start | bytes 1540
  191.5 1.0 copy-start.6
  193.0 3.4 copy-start.2
  193.1 3.4 copy-start.7
  195.5 0.8 copy-start.9
  195.6 0.9 copy-start.10
  249.0 15.0 %copy-start.4 = (pred[128,4096]{0,1:T(8,128)(4,1)S(1)}, pred[128,4096]{0,1:T(8,128)(4,1)}, u32[]{:S(2)}) copy-start(pred[128,4096]{0,1:T(8,128)(4,1)} %fusion.29) | copy-start | bytes 1572868
  263.9 20.3 %copy-start.1 = (f32[2,128,8,4096]{3,1,2,0:T(8,128)S(1)}, f32[2,128,8,4096]{3,1,2,0:T(8,128)}, u32[]{:S(2)}) copy-start(f32[2,128,8,4096]{3,1,2,0:T(8,128)} %get-tuple-element.20) | copy-start | bytes 100663296
  264.0 20.3 %copy-start.3 = (pred[128,4096]{1,0:T(8,128)(4,1)S(1)}, pred[128,4096]{1,0:T(8,128)(4,1)}, u32[]{:S(2)}) copy-start(pred[128,4096]{1,0:T(8,128)(4,1)} %broadcast_compare_fusion) | copy-start | bytes 1572868
  429.0 6.0 copy-start.19
  433.9 1.0 copy-start.5
  604.9 7.7 %copy-start.20 = (f32[128,8]{0,1:T(8,128)S(1)}, f32[128,8]{0,1:T(8,128)}, u32[]{:S(2)}) copy-start(f32[128,8]{0,1:T(8,128)} %param.29) | copy-start | bytes 12292
  604.9 7.8 %copy-start.13 = (bf16[128,2,64]{2,0,1:T(8,128)(2,1)S(1)}, bf16[128,2,64]{2,0,1:T(8,128)(2,1)}, u32[]{:S(2)}) copy-start(bf16[128,2,64]{2,0,1:T(8,128)(2,1)} %copy-done.12) | copy-start | bytes 98308
  604.9 7.8 %copy-start.15 = (bf16[128,2,64]{2,0,1:T(8,128)(2,1)S(1)}, bf16[128,2,64]{2,0,1:T(8,128)(2,1)}, u32[]{:S(2)}) copy-start(bf16[128,2,64]{2,0,1:T(8,128)(2,1)} %copy-done.14) | copy-start | bytes 98308
  604.9 7.9 %copy-start.17 = (bf16[128,256]{1,0:T(8,128)(2,1)S(1)}, bf16[128,256]{1,0:T(8,128)(2,1)}, u32[]{:S(2)}) copy-start(bf16[128,256]{1,0:T(8,128)(2,1)} %copy-done.16) | copy-start | bytes 196612
  604.9 112.6 %all-to-all-start.1 = ((bf16[128,12,2048]{2,1,0:T(8,128)(2,1)}), bf16[128,12,2048]{2,1,0:T(8,128)(2,1)}, u32[]{:S(2)}, u32[]{:S(2)}) async-start(bf16[128,12,2048]{2,1,0:T(8,128)(2,1)} %reshape.352), calls=%async_computation.1 | async-start | bytes 16777216 | tf_op jit(solution)/shard_map/all_to_all | solution.py:201
Sparse Core Ops, SparseCore 0:
  11.1 117.4 all-gather.5
  130.2 45.2 all-gather.11
  179.3 69.6 all-gather.7
  251.6 71.0 all-gather.9
  325.6 103.2 all-gather.13
where the time goes:
time: 762 us; the launch traced here: 756 us
  waiting for transfers between devices  382 us (50%)
  blocking collectives  105 us (14%)
  local copies, waits for them, and re-layouts  102 us (13%)
  matrix products  93.2 us (12%)
  other arithmetic  51.6 us (7%)
  between operations  14.5 us (2%)
  starting transfers between devices  7.85 us (1%)
    all_gather x1, waiting for transfers between devices, local(): lax.all_gather(query_key_value_weight, 'expert', axis=0, tiled=True)  114 us
    all_to_all x1, blocking collectives, local(): lax.all_to_all(outgoing.reshape(expert_count, capacity, width), ('dp', 'e...  105 us
    all_to_all x1, waiting for transfers between devices, local(): lax.all_to_all(results, ('dp', 'expert'), split_axis=0, concat_axis=0, ti...  104 us
    all_gather x1, waiting for transfers between devices, local(): lax.all_gather(w_out, 'expert', axis=0, tiled=True)  73.6 us
    all_gather x1, waiting for transfers between devices, local(): piece_keys = lax.all_gather(key_rows, 'expert', axis=0, tiled=True)  38.8 us
    dot_general x2, matrix products, attend(): jnp.einsum('kgqs,skd->kgqd', weights.astype(jnp.bfloat16), value_rows, pr...  32.7 us
    all_gather x1, waiting for transfers between devices, local(): piece_values = lax.all_gather(value_rows, 'expert', axis=0, tiled=True)  28.9 us
    dot_general x2, matrix products, attend(): jnp.einsum('qkgd,skd->kgqs', queries, key_rows, preferred_element_type=jn...  28.6 us
  transfers between devices with their start and end apart: 6, of which 6 were waited for; matrix products, arithmetic and copies ran while one was open for 18% of the time, Pallas kernels for 0%

commit v1 on v0

--- a/solution.py
+++ b/solution.py
@@ -102,7 +102,15 @@
     part = normed
     qkv = jnp.dot(
         part,
-        lax.all_gather(query_key_value_weight, "expert", axis=0, tiled=True),
+        jnp.concatenate(
+            lax.all_to_all(
+                jnp.stack([query_key_value_weight for _ in range(lax.axis_size("expert"))], axis=0),
+                "expert",
+                0,
+                0,
+            ),
+            axis=0,
+        ),
         preferred_element_type=jnp.float32,
     )
     index = col * tokens_here + jnp.arange(tokens_here, dtype=jnp.int32)

time: 762 us -> 810 us (1.063)
  waiting for transfers between devices: 382 us -> 415 us
  starting transfers between devices: 7.85 us -> 16.7 us
    all_to_all x0 -> x1, waiting for transfers between devices: none -> 178 us  [local(): lax.all_to_all(jnp.stack([query_key_value_weight for _ in range(lax.axis_...]
    all_gather x1 -> x0, waiting for transfers between devices: 114 us -> none  [local(): lax.all_gather(query_key_value_weight, 'expert', axis=0, tiled=True)]
    all_gather x1, waiting for transfers between devices: 21.2 us -> 0.01 us  [local(): piece = lax.all_gather(kv_pool, 'dp', axis=0, tiled=True)]
    all_gather x1, waiting for transfers between devices: 38.8 us -> 29.7 us  [local(): piece_keys = lax.all_gather(key_rows, 'expert', axis=0, tiled=True)]
    all_to_all x0 -> x1, starting transfers between devices: none -> 8.93 us  [local(): lax.all_to_all(jnp.stack([query_key_value_weight for _ in range(lax.axis_...]
  transfers between devices with their start and end apart: 6 -> 6, of which waited for: 6 -> 5; matrix products, arithmetic and copies ran while one was open for 18% -> 17% of each run, Pallas kernels for 0% -> 0%
where the time goes in v1:
time: 810 us; the launch traced here: 803 us
  waiting for transfers between devices  415 us (51%)
  local copies, waits for them, and re-layouts  107 us (13%)
  blocking collectives  105 us (13%)
  matrix products  93.2 us (12%)
  other arithmetic  51.6 us (6%)
  starting transfers between devices  16.7 us (2%)
  between operations  14.5 us (2%)
    all_to_all x1, waiting for transfers between devices, local(): lax.all_to_all(jnp.stack([query_key_value_weight for _ in range(lax.axis_...  178 us
    all_to_all x1, blocking collectives, local(): lax.all_to_all(outgoing.reshape(expert_count, capacity, width), ('dp', 'e...  105 us
    all_to_all x1, waiting for transfers between devices, local(): lax.all_to_all(results, ('dp', 'expert'), split_axis=0, concat_axis=0, ti...  104 us
    all_gather x1, waiting for transfers between devices, local(): lax.all_gather(w_out, 'expert', axis=0, tiled=True)  73.6 us
    dot_general x2, matrix products, attend(): jnp.einsum('kgqs,skd->kgqd', weights.astype(jnp.bfloat16), value_rows, pr...  32.7 us
    all_gather x1, waiting for transfers between devices, local(): piece_keys = lax.all_gather(key_rows, 'expert', axis=0, tiled=True)  29.7 us
    all_gather x1, waiting for transfers between devices, local(): piece_values = lax.all_gather(value_rows, 'expert', axis=0, tiled=True)  29 us
    dot_general x2, matrix products, attend(): jnp.einsum('qkgd,skd->kgqs', queries, key_rows, preferred_element_type=jn...  28.7 us
  transfers between devices with their start and end apart: 6, of which 5 were waited for; matrix products, arithmetic and copies ran while one was open for 17% of the time, Pallas kernels for 0%

profile of v1, /device:TPU:67, one launch (start us, length us, event | category | flops | bytes accessed | tf_op | source)
XLA Modules:
  0.0 803.5 jit_solution(7303006617059966330)
XLA Ops:
  7.2 6.1 stack.2
  13.3 8.9 %all-to-all-start = ((bf16[32,64,2560]{2,1,0:T(8,128)(2,1)}), bf16[32,64,2560]{2,1,0:T(8,128)(2,1)}, u32[]{:S(2)}, u32[]{:S(2)}) async-start(bf16[32,64,2560]{2,1,0:T(8,128)(2,1)} %stack.2), calls=%async_computation | async-start | bytes 20971520 | tf_op jit(solution)/shard_map/all_to_all | solution.py:106
  22.3 2.6 copy.97
  26.0 1.2 fusion.65
  27.6 178.4 %all-to-all-done = bf16[32,64,2560]{2,1,0:T(8,128)(2,1)} async-done(((bf16[32,64,2560]{2,1,0:T(8,128)(2,1)}), bf16[32,64,2560]{2,1,0:T(8,128)(2,1)}, u32[]{:S(2)}, u32[]{:S(2)}) %all-to-all-start) | async-done | bytes 10485792 | tf_op jit(solution)/shard_map/all_to_all | solution.py:106
  206.0 5.8 fusion.68
  211.7 1.1 copy-done.8
  213.5 1.6 reshape.351
  215.1 1.1 multiply_reduce_fusion.2
  218.0 0.9 slice.85
  221.7 1.9 broadcast_add_fusion
  223.8 1.9 copy.104
  226.0 1.4 fusion.71
  227.4 1.2 broadcast_compare_fusion
  228.6 3.1 fusion.29
  231.7 4.1 fusion.94
  235.8 1.6 copy.98
  237.4 4.6 copy.99
  242.0 4.2 reshape.380
  246.2 1.3 slice_bitcast_fusion
  247.7 1.0 copy-done.6
  249.3 1.7 multiply_multiply_fusion
  252.7 13.7 %bitcast_reduce_fusion = (f32[2,8,128]{2,1,0:T(8,128)S(1)}, f32[2,128,8,4096]{3,1,2,0:T(8,128)}) fusion(pred[128,4096]{1,0:T(8,128)(4,1)S(1)} %copy-done.2, bf16[4096,2,128,1]{2,0,3,1:T(8,128)(2,1)S(1)} %bitcast.169, bf16[128,2,8,64]{3,0,2,1:T(8,128)(2,1)S(1)} %bitcast.172, bf16[128,2,8,64]{3,0,2,1:T(8,128)(2,1)S(1)} %bitcast.170), kind=kOutput, calls=%fused_computation.3 | convolution fusion | flops 2173696000 | bytes 36708352 | tf_op jit(solution)/shard_map/qkgd,skd->kgqs/dot_general | solution.py:48
  266.4 29.7 %all-gather.5.cloned.1.call-done = bf16[4096,2,128]{2,0,1:T(8,128)(2,1)} async-done(((bf16[128,2,128]{2,0,1:T(8,128)(2,1)}), bf16[4096,2,128]{2,0,1:T(8,128)(2,1)}) %all-gather.5.cloned.1.call-update) | async-done | bytes 2097168 | tf_op jit(solution)/shard_map/all_gather | solution.py:153
  296.2 15.0 %fusion.3 = (f32[2,8,128]{2,1,0:T(8,128)S(1)}, f32[2,4096,128,8]{2,1,3,0:T(8,128)}) fusion(pred[128,4096]{0,1:T(8,128)(4,1)} %fusion.29, bf16[128,2,8,64]{3,0,2,1:T(8,128)(2,1)} %bitcast.173, bf16[128,2,8,64]{3,0,2,1:T(8,128)(2,1)} %bitcast.171, bf16[4096,2,128]{2,0,1:T(8,128)(2,1)} %all-gather.5.cloned.1.call-done), kind=kOutput, calls=%fused_computation.10 | convolution fusion | flops 2173696000 | bytes 36708352 | tf_op jit(solution)/shard_map/qkgd,skd->kgqs/dot_general | solution.py:48
  311.1 16.4 %fusion.1 = f32[2,8,128]{2,1,0:T(8,128)S(1)} fusion(f32[2,4096,128,8]{2,1,3,0:T(8,128)} %get-tuple-element.22, f32[2,8,128]{2,1,0:T(8,128)S(1)} %get-tuple-element.16, pred[128,4096]{0,1:T(8,128)(4,1)S(1)} %copy-done.4), kind=kLoop, calls=%fused_computation.8 | loop fusion | flops 33552384 | bytes 34095104 | tf_op jit(solution)/shard_map/reduce_sum | solution.py:54
  327.5 3.9 copy-done.1
  331.4 9.5 %fusion.4 = f32[2,8,128]{2,1,0:T(8,128)S(1)} fusion(f32[2,128,8,4096]{3,1,2,0:T(8,128)S(1)} %copy-done.1, f32[2,8,128]{2,1,0:T(8,128)S(1)} %get-tuple-element.15, pred[128,4096]{1,0:T(8,128)(4,1)S(1)} %copy-done.3), kind=kLoop, calls=%fused_computation.11 | loop fusion | flops 33552384 | bytes 34095104 | tf_op jit(solution)/shard_map/reduce_sum | solution.py:54
  341.0 29.0 %all-gather.7.cloned.1.call-done = bf16[4096,2,128]{0,2,1:T(8,128)(2,1)} async-done(((bf16[128,2,128]{0,2,1:T(8,128)(2,1)}), bf16[4096,2,128]{0,2,1:T(8,128)(2,1)}) %all-gather.7.cloned.1.call-update) | async-done | bytes 2097168 | tf_op jit(solution)/shard_map/all_gather | solution.py:154
  370.0 16.3 %fusion.50 = f32[128,2,8,128]{0,3,2,1:T(8,128)} fusion(f32[2,4096,128,8]{2,1,3,0:T(8,128)} %get-tuple-element.22, f32[2,8,128]{2,1,0:T(8,128)S(1)} %get-tuple-element.16, pred[128,4096]{0,1:T(8,128)(4,1)} %fusion.29, bf16[4096,2,128]{0,2,1:T(8,128)(2,1)} %all-gather.7.cloned.1.call-done, f32[128,2,8]{0,2,1:T(8,128)S(1)} %get-tuple-element.5, ...), kind=kOutput, calls=%fused_computation.45 | convolution fusion | flops 2181562368 | bytes 37249024 | tf_op jit(solution)/shard_map/kgqs,skd->kgqd/dot_general | solution.py:55
  386.3 16.3 %fusion.60 = bf16[128,2,8,128]{0,3,2,1:T(8,128)(2,1)} fusion(f32[128,2,8,128]{0,3,2,1:T(8,128)} %fusion.50, bf16[4096,2,128,1]{0,2,1,3:T(8,128)(2,1)} %reshape.380, f32[2,128,8,4096]{3,1,2,0:T(8,128)} %get-tuple-element.20, f32[2,8,128]{2,1,0:T(8,128)S(1)} %get-tuple-element.15, pred[128,4096]{1,0:T(8,128)(4,1)} %broadcast_compare_fusion, ...), kind=kOutput, calls=%fused_computation.47 | convolution fusion | flops 2181824512 | bytes 37765120 | tf_op jit(solution)/shard_map/kgqs,skd->kgqd/dot_general | solution.py:55
  402.7 73.6 %all-gather.11.cloned.1.call-done = bf16[2048,2048]{1,0:T(8,128)(2,1)} async-done(((bf16[64,2048]{1,0:T(8,128)(2,1)}), bf16[2048,2048]{1,0:T(8,128)(2,1)}) %all-gather.11.cloned.1.call-update) | async-done | bytes 8388624 | tf_op jit(solution)/shard_map/all_gather | solution.py:185
  476.3 4.9 multiply_reduce_fusion
  481.2 1.0 copy-done.5
  482.2 0.9 multiply_convert_fusion
  483.2 10.9 %scatter_custom_fusion = bf16[1536,2048]{1,0:T(8,128)(2,1)} fusion(s32[1024]{0:T(1024)S(1)} %bitcast.177, bf16[]{:T(256)} %constant.80.clone.1, bf16[128,2048]{1,0:T(8,128)(2,1)} %multiply_convert_fusion), kind=kCustom, calls=%fused_computation.24 | custom fusion | bytes 6815746 | tf_op jit(solution)/shard_map/scatter | solution.py:198
  494.1 10.6 %reshape.356 = bf16[128,12,2048]{2,1,0:T(8,128)(2,1)} reshape(bf16[1536,2048]{1,0:T(8,128)(2,1)} %scatter_custom_fusion) | data formatting | bytes 12582912 | tf_op jit(solution)/shard_map/reshape | solution.py:202
  504.7 105.0 %all_to_all.15 = bf16[128,12,2048]{2,1,0:T(8,128)(2,1)} all-to-all(bf16[128,12,2048]{2,1,0:T(8,128)(2,1)} %reshape.356), channel_id=1, replica_groups=mesh['dp'=4,'expert'=32] {'dp','expert'}, dimensions={0} | all-to-all | bytes 12582912 | tf_op jit(solution)/shard_map/all_to_all | solution.py:201
  609.7 10.7 %reshape.357 = bf16[1536,2048]{1,0:T(8,128)(2,1)} reshape(bf16[128,12,2048]{2,1,0:T(8,128)(2,1)} %all_to_all.15) | data formatting | bytes 12582912 | tf_op jit(solution)/shard_map/reshape | solution.py:208
  620.4 14.1 %fusion.13 = f32[1536,1536]{1,0:T(8,128)S(1)} fusion(bf16[1536,2048]{1,0:T(8,128)(2,1)} %reshape.357, bf16[1,2048,1536]{2,1,0:T(8,128)(2,1)} %param.22), kind=kOutput, calls=%fused_computation.20 | convolution fusion | flops 9663676416 | bytes 22020096 | tf_op jit(solution)/shard_map/dot_general | solution.py:65
  634.6 7.1 convolution_convert_fusion
  641.6 10.6 %reshape.358 = bf16[128,12,2048]{2,1,0:T(8,128)(2,1)} reshape(bf16[1536,2048]{1,0:T(8,128)(2,1)} %convolution_convert_fusion) | data formatting | bytes 12582912 | tf_op jit(solution)/shard_map/reshape | solution.py:208
  652.2 7.6 all-to-all-start.2
  660.8 104.1 %all-to-all-done.2 = bf16[128,12,2048]{2,1,0:T(8,128)(2,1)} async-done(((bf16[128,12,2048]{2,1,0:T(8,128)(2,1)}), bf16[128,12,2048]{2,1,0:T(8,128)(2,1)}, u32[]{:S(2)}, u32[]{:S(2)}) %all-to-all-start.2) | async-done | bytes 6291488 | tf_op jit(solution)/shard_map/all_to_all | solution.py:209
  764.8 10.7 %reshape.359 = bf16[1536,2048]{1,0:T(8,128)(2,1)} reshape(bf16[128,12,2048]{2,1,0:T(8,128)(2,1)} %all-to-all-done.2) | data formatting | bytes 12582912 | tf_op jit(solution)/shard_map/reshape | solution.py:210
  775.5 12.4 %gather_fusion = bf16[1024,2048]{1,0:T(8,128)(2,1)} fusion(bf16[1536,2048]{1,0:T(8,128)(2,1)} %reshape.359, s32[1024]{0:T(1024)S(1)} %broadcast_clamp_fusion), kind=kCustom, calls=%fused_computation | custom fusion | bytes 8392704 | tf_op jit(solution)/shard_map/gather | solution.py:210
  788.0 6.5 fusion.12
  794.5 2.2 add_convert_fusion
  (105 shorter events, 10.5 us)
Async XLA Ops:
  7.2 627.4 %copy-start = (bf16[1,768,2048]{2,1,0:T(8,128)(2,1)S(1)}, bf16[1,768,2048]{2,1,0:T(8,128)(2,1)}, u32[]{:S(2)}) copy-start(bf16[1,768,2048]{2,1,0:T(8,128)(2,1)} %param.23) | copy-start | bytes 9437188
  13.3 11.6 %copy-start.24 = (s32[4,4]{1,0:T(4,128)S(1)}, s32[4,4]{1,0:T(4,128)}, u32[]{:S(2)}) copy-start(s32[4,4]{1,0:T(4,128)} %param.26) | copy-start | bytes 196
  13.3 192.6 %copy-start.18 = (f32[2048]{0:T(1024)S(1)}, f32[2048]{0:T(1024)}, u32[]{:S(2)}) copy-start(f32[2048]{0:T(1024)} %param.16) | copy-start | bytes 24580
  13.3 192.6 %all-to-all-start = ((bf16[32,64,2560]{2,1,0:T(8,128)(2,1)}), bf16[32,64,2560]{2,1,0:T(8,128)(2,1)}, u32[]{:S(2)}, u32[]{:S(2)}) async-start(bf16[32,64,2560]{2,1,0:T(8,128)(2,1)} %stack.2), calls=%async_computation | async-start | bytes 20971520 | tf_op jit(solution)/shard_map/all_to_all | solution.py:106
  22.3 209.4 %all-gather.9.cloned.1.call-start = ((), (), s32[]{:S(2)}) async-start(), calls=%async_computation.5 | async-start | bytes 5242880 | tf_op jit(solution)/shard_map/all_gather | solution.py:161
  24.9 271.3 %all-gather.5.cloned.1.call-start = ((), (), s32[]{:S(2)}) async-start(), calls=%async_computation.3 | async-start | bytes 2162688 | tf_op jit(solution)/shard_map/all_gather | solution.py:153
  205.9 10.4 %copy-start.22 = (f32[128]{0:T(128)S(1)}, f32[128]{0:T(128)}, u32[]{:S(2)}) copy-start(f32[128]{0:T(128)} %param.19) | copy-start | bytes 1540
  206.0 14.4 %copy-start.19 = (s32[128,8]{0,1:T(8,128)S(1)}, s32[128,8]{0,1:T(8,128)}, u32[]{:S(2)}) copy-start(s32[128,8]{0,1:T(8,128)} %param.28) | copy-start | bytes 12292
  206.0 17.7 %copy-start.25 = (s32[32]{0:T(128)S(1)}, s32[32]{0:T(128)}, u32[]{:S(2)}) copy-start(s32[32]{0:T(128)} %param.25) | copy-start | bytes 388
  211.7 1.1 copy-start.8
  216.6 0.6 copy-start.12
  216.6 0.6 copy-start.14
  218.0 152.0 %all-gather.7.cloned.1.call-start = ((), (), s32[]{:S(2)}) async-start(), calls=%async_computation.4 | async-start | bytes 2162688 | tf_op jit(solution)/shard_map/all_gather | solution.py:154
  218.9 1.3 copy-start.16
  219.7 256.6 %all-gather.11.cloned.1.call-start = ((), (), s32[]{:S(2)}) async-start(), calls=%async_computation.6 | async-start | bytes 8650752 | tf_op jit(solution)/shard_map/all_gather | solution.py:185
  220.9 0.8 copy-start.11
  235.8 13.5 %copy-start.23 = (f32[128]{0:T(128)S(1)}, f32[128]{0:T(128)}, u32[]{:S(2)}) copy-start(f32[128]{0:T(128)} %param.18) | copy-start | bytes 1540
  247.7 1.0 copy-start.6
  249.3 3.4 copy-start.2
  249.3 3.4 copy-start.7
  251.7 0.8 copy-start.9
  251.8 0.9 copy-start.10
  296.2 15.0 %copy-start.4 = (pred[128,4096]{0,1:T(8,128)(4,1)S(1)}, pred[128,4096]{0,1:T(8,128)(4,1)}, u32[]{:S(2)}) copy-start(pred[128,4096]{0,1:T(8,128)(4,1)} %fusion.29) | copy-start | bytes 1572868
  311.1 20.3 %copy-start.1 = (f32[2,128,8,4096]{3,1,2,0:T(8,128)S(1)}, f32[2,128,8,4096]{3,1,2,0:T(8,128)}, u32[]{:S(2)}) copy-start(f32[2,128,8,4096]{3,1,2,0:T(8,128)} %get-tuple-element.20) | copy-start | bytes 100663296
  311.1 20.3 %copy-start.3 = (pred[128,4096]{1,0:T(8,128)(4,1)S(1)}, pred[128,4096]{1,0:T(8,128)(4,1)}, u32[]{:S(2)}) copy-start(pred[128,4096]{1,0:T(8,128)(4,1)} %broadcast_compare_fusion) | copy-start | bytes 1572868
  476.3 6.0 copy-start.20
  481.2 1.0 copy-start.5
  652.2 7.7 copy-start.21
  652.2 7.8 copy-start.13
  652.2 7.8 copy-start.15
  652.2 7.9 copy-start.17
  652.2 112.6 %all-to-all-start.2 = ((bf16[128,12,2048]{2,1,0:T(8,128)(2,1)}), bf16[128,12,2048]{2,1,0:T(8,128)(2,1)}, u32[]{:S(2)}, u32[]{:S(2)}) async-start(bf16[128,12,2048]{2,1,0:T(8,128)(2,1)} %reshape.358), calls=%async_computation.2 | async-start | bytes 16777216 | tf_op jit(solution)/shard_map/all_to_all | solution.py:209
Sparse Core Ops, SparseCore 0:
  25.0 83.8 all-gather.8
  218.1 78.0 all-gather.4
  298.9 71.0 all-gather.6
  372.9 103.2 all-gather.10
